TPU v7x, 128 devices: a whole 4x4x4 slice. The times are simulated.
128 devices in a mesh: slab: 16 (over y, x), grp: 8 (over z, core).
Axes of the slice: x: 4, y: 4, z: 4, core: 2. Of those that a mesh axis runs over, the one named last changes fastest.
Arguments:
- initial: float32 [32, 64, 32, 256], P('grp', 'slab'), may hold values from 0 to 1
- target: float32 [32, 64, 32, 256], P('grp', 'slab'), may hold values from 0 to 0.6
- birth_step: int32 [64, 32, 256], P('slab'), may hold values from 0 to 4, as said below
- classes: int32 [32], P('grp'), may hold values from 0 to 3
- mobility: float32 [4, 4], replicated, may hold values from 0.2 to 2
Outputs:
- final_state: float32 [32, 64, 32, 256], P('grp', 'slab')
- initial_grad: float32 [32, 64, 32, 256], P('grp', 'slab')
- mobility_grad: float32 [4, 4], replicated
Inputs may be any that keep to these rules, and one draw needn't show every extreme that they name: A voxel takes part in step n when birth_step <= n; the value 4 means that it never takes part in the window; exactly one voxel has the value 0.
All inputs are finite; a program needn't handle non-finite values.
Results may differ from a plain program's by a relative error of at most 0.0001.
Values sent between devices are 32-bit elements; how exact they have to be, the bound alone decides.
No kernel may reach another device: no remote copies, remote signals or barrier semaphores. Data moves between devices by JAX's collectives and lax.ppermute only.
A program may use at most 64 MiB of HBM per device.

v0:
```python
import jax
import jax.numpy as jnp
from jax import lax
from jax.sharding import PartitionSpec as P

STEPS = 4
coupling = 0.3
stiffness = 1.0
time_step = 0.06


def extended_2(cells, sides, width):
    for axis, dim in sides:
        count = lax.axis_size(axis)
        ends = count - 1
        head = lax.slice_in_dim(cells, 0, width, axis=dim)
        tail = lax.slice_in_dim(cells, cells.shape[dim] - width, cells.shape[dim], axis=dim)
        cells = jnp.concatenate(
            [
                lax.ppermute(tail, axis, [(i, (i + 1) % count) for i in range(ends)]),
                cells,
                lax.ppermute(head, axis, [((i + 1) % count, i) for i in range(ends)]),
            ],
            axis=dim,
        )
    return cells


def laplace_local(extended):
    padded = jnp.pad(extended, ((0, 0), (0, 0), (1, 1), (1, 1)))
    centre = padded[:, 1:-1, 1:-1, 1:-1]
    return (
        padded[:, 2:, 1:-1, 1:-1]
        + padded[:, :-2, 1:-1, 1:-1]
        + padded[:, 1:-1, 2:, 1:-1]
        + padded[:, 1:-1, :-2, 1:-1]
        + padded[:, 1:-1, 1:-1, 2:]
        + padded[:, 1:-1, 1:-1, :-2]
        - 6.0 * centre
    )


def advance_local(fields, pair_rates, member, active):
    squared = fields * fields
    partial_sums = jnp.einsum("pk,pxzy->kxzy", member, squared, precision=lax.Precision.HIGHEST)
    class_sums = lax.psum(partial_sums, "grp")
    summed = jnp.sum(class_sums, axis=0)
    inverse = 1.0 / (1.0 + summed)
    driving = jnp.einsum("pk,kxzy->pxzy", pair_rates, class_sums, precision=lax.Precision.HIGHEST)
    rates = driving * inverse[None]
    extended = extended_2(fields, (("slab", 1),), 1)
    potential = (
        -fields
        + fields * squared
        + 2.0 * coupling * fields * (summed[None] - squared)
        - stiffness * laplace_local(extended)
    )
    weighted = active[None] * rates
    numerator, raw_denominator = lax.psum(
        (jnp.sum(weighted * potential, axis=(1, 2, 3)), jnp.sum(weighted, axis=(1, 2, 3))), "slab"
    )
    lagrange = numerator / jnp.maximum(raw_denominator, 1.0)
    updated = fields - time_step * weighted * (potential - lagrange[:, None, None, None])
    return (updated, potential, class_sums, numerator, raw_denominator)


def retreat(
    state_adj_next,
    fields,
    potential,
    class_sums,
    numerator,
    raw_denominator,
    member,
    pair_rates,
    active,
):
    squared = fields * fields
    summed = jnp.sum(class_sums, axis=0)
    inverse = 1.0 / (1.0 + summed)
    driving = jnp.einsum("pk,kxzy->pxzy", pair_rates, class_sums, precision=lax.Precision.HIGHEST)
    rates = driving * inverse[None]
    weighted = active[None] * rates
    denominator = jnp.maximum(raw_denominator, 1.0)
    lagrange = numerator / denominator
    scaled = time_step * active[None] * state_adj_next
    first_part = scaled * rates
    lagrange_adj = lax.psum(jnp.sum(first_part, axis=(1, 2, 3)), "slab")
    numer_adj = lagrange_adj / denominator
    potential_adj = weighted * numer_adj[:, None, None, None] - first_part
    extended = extended_2(potential_adj, (("slab", 1),), 1)
    curvature = laplace_local(extended)
    denom_adj = jnp.where(
        raw_denominator > 1.0, -lagrange_adj * numerator / (denominator * denominator), 0.0
    )
    rate_adj = -scaled * (potential - lagrange[:, None, None, None]) + active[None] * (
        numer_adj[:, None, None, None] * potential + denom_adj[:, None, None, None]
    )
    drive_adj = rate_adj * inverse[None]
    state_adj = (
        state_adj_next
        + potential_adj
        * (
            -1.0
            + 3.0 * squared
            + 2.0 * coupling * (summed[None] - squared)
            - 4.0 * coupling * squared
        )
        - stiffness * curvature
    )
    weighted_sums = jnp.einsum(
        "pk,pxzy->kxzy", pair_rates, drive_adj, precision=lax.Precision.HIGHEST
    )
    shared_sum = jnp.sum(
        2.0 * coupling * potential_adj * fields - (inverse * inverse)[None] * rate_adj * driving,
        axis=0,
    )
    weighted_sums, shared_sum = lax.psum((weighted_sums, shared_sum), "grp")
    class_adj = weighted_sums + shared_sum[None]
    state_adj = state_adj + 2.0 * fields * jnp.einsum(
        "pk,kxzy->pxzy", member, class_adj, precision=lax.Precision.HIGHEST
    )
    products = jnp.einsum("pxzy,kxzy->pk", drive_adj, class_sums, precision=lax.Precision.HIGHEST)
    mobility_term = jnp.dot(member.T, products, precision=lax.Precision.HIGHEST)
    return (state_adj, mobility_term)


def on_device(initial, target, birth_step, classes, mobility):
    classes_count = mobility.shape[0]
    member = (classes[:, None] == jnp.arange(classes_count, dtype=jnp.int32)[None, :]).astype(
        jnp.float32
    )
    pair_rates = jnp.dot(member, mobility, precision=lax.Precision.HIGHEST)
    fields = initial
    stored = []
    for step_index in range(STEPS):
        active = (birth_step <= step_index).astype(jnp.float32)
        updated, potential, class_sums, numerator, raw_denominator = advance_local(
            fields, pair_rates, member, active
        )
        stored.append((fields, potential, class_sums, numerator, raw_denominator, active))
        fields = updated
    state_adj = fields - target
    mobility_acc = jnp.zeros((classes_count, classes_count), jnp.float32)
    for step_index in range(STEPS - 1, -1, -1):
        saved_fields, potential, class_sums, numerator, raw_denominator, active = stored[step_index]
        state_adj, mobility_term = retreat(
            state_adj,
            saved_fields,
            potential,
            class_sums,
            numerator,
            raw_denominator,
            member,
            pair_rates,
            active,
        )
        mobility_acc = mobility_acc + mobility_term
    mobility_total = lax.psum(mobility_acc, ("slab", "grp"))
    scale = time_step * (initial.shape[1] * lax.axis_size("slab")) * initial.shape[2]
    return (fields, state_adj, mobility_total / scale)


def solution(mesh):
    return jax.shard_map(
        on_device,
        mesh=mesh,
        in_specs=(
            P("grp", "slab", None, None),
            P("grp", "slab", None, None),
            P("slab", None, None),
            P("grp"),
            P(),
        ),
        out_specs=(P("grp", "slab", None, None), P("grp", "slab", None, None), P()),
        check_vma=False,
    )
```

profile of v0, /device:TPU:0, one launch (start us, length us, event | category | flops | bytes accessed | tf_op | source)
XLA Modules:
  0.0 990.1 jit_solution(4415834130746513272)
XLA Ops:
  20.0 60.5 %all-reduce.25.cloned.1.call-done = f32[4,4,32,256]{3,0,2,1:T(4,128)} async-done(((f32[4,4,32,256]{3,0,2,1:T(4,128)}), f32[4,4,32,256]{3,0,2,1:T(4,128)}) %all-reduce.25.cloned.1.call-update) | async-done | bytes 524304 | tf_op jit(solution)/shard_map/psum | solution.py:46
  85.7 40.3 %all-reduce.11 = (f32[4]{0:T(128)S(1)}, f32[4]{0:T(128)S(1)}) all-reduce(f32[4]{0:T(128)S(1)} %get-tuple-element.13, f32[4]{0:T(128)S(1)} %get-tuple-element.12), channel_id=1, replica_groups=mesh['slab'=16,'grp'=8] {'slab'}, use_global_device_ids=true, to_apply=%region_3.4 | all-reduce | flops 8 | bytes 64 | tf_op jit(solution)/shard_map/psum | solution.py:59
  138.2 52.1 %all-reduce.27.cloned.1.call-done = f32[4,4,32,256]{3,0,2,1:T(4,128)} async-done(((f32[4,4,32,256]{3,0,2,1:T(4,128)}), f32[4,4,32,256]{3,0,2,1:T(4,128)}) %all-reduce.27.cloned.1.call-update) | async-done | bytes 524304 | tf_op jit(solution)/shard_map/psum | solution.py:46
  196.5 40.3 %all-reduce.10 = (f32[4]{0:T(128)S(1)}, f32[4]{0:T(128)S(1)}) all-reduce(f32[4]{0:T(128)S(1)} %get-tuple-element.11, f32[4]{0:T(128)S(1)} %get-tuple-element.10), channel_id=1, replica_groups=mesh['slab'=16,'grp'=8] {'slab'}, use_global_device_ids=true, to_apply=%region_9.10 | all-reduce | flops 8 | bytes 64 | tf_op jit(solution)/shard_map/psum | solution.py:59
  247.7 52.0 %all-reduce.29.cloned.1.call-done = f32[4,4,32,256]{3,0,2,1:T(4,128)} async-done(((f32[4,4,32,256]{3,0,2,1:T(4,128)}), f32[4,4,32,256]{3,0,2,1:T(4,128)}) %all-reduce.29.cloned.1.call-update) | async-done | bytes 524304 | tf_op jit(solution)/shard_map/psum | solution.py:46
  301.8 4.6 fusion.136
  306.4 40.4 %all-reduce.9 = (f32[4]{0:T(128)S(1)}, f32[4]{0:T(128)S(1)}) all-reduce(f32[4]{0:T(128)} %get-tuple-element.9, f32[4]{0:T(128)} %get-tuple-element.8), channel_id=1, replica_groups=mesh['slab'=16,'grp'=8] {'slab'}, use_global_device_ids=true, to_apply=%region_15.16 | all-reduce | flops 8 | bytes 64 | tf_op jit(solution)/shard_map/psum | solution.py:59
  359.5 51.8 %all-reduce.31.cloned.1.call-done = f32[4,4,32,256]{3,0,2,1:T(4,128)} async-done(((f32[4,4,32,256]{3,0,2,1:T(4,128)}), f32[4,4,32,256]{3,0,2,1:T(4,128)}) %all-reduce.31.cloned.1.call-update) | async-done | bytes 524304 | tf_op jit(solution)/shard_map/psum | solution.py:46
  413.4 5.4 fusion.137
  418.8 40.4 %all-reduce.8 = (f32[4]{0:T(128)S(1)}, f32[4]{0:T(128)S(1)}) all-reduce(f32[4]{0:T(128)} %get-tuple-element.7, f32[4]{0:T(128)} %get-tuple-element.6), channel_id=1, replica_groups=mesh['slab'=16,'grp'=8] {'slab'}, use_global_device_ids=true, to_apply=%region_21.22 | all-reduce | flops 8 | bytes 64 | tf_op jit(solution)/shard_map/psum | solution.py:59
  462.4 35.5 %psum.187 = f32[4]{0:T(128)S(1)} all-reduce(f32[4]{0:T(128)S(1)} %get-tuple-element.48), channel_id=1, replica_groups=mesh['slab'=16,'grp'=8] {'slab'}, use_global_device_ids=true, to_apply=%region_25.26 | all-reduce | flops 4 | bytes 32 | tf_op jit(solution)/shard_map/psum | solution.py:88
  501.9 4.5 collective-permute-start.9
  518.2 50.4 %all-reduce.39.cloned.1.call-done = (f32[4,4,32,256]{3,0,2,1:T(4,128)}, f32[4,32,256]{2,1,0:T(8,128)}) async-done(((f32[4,4,32,256]{3,0,2,1:T(4,128)}, f32[4,32,256]{2,1,0:T(8,128)}), (f32[4,4,32,256]{3,0,2,1:T(4,128)}, f32[4,32,256]{2,1,0:T(8,128)})) %all-reduce.39.cloned.1.call-update) | async-done | bytes 655376 | tf_op jit(solution)/shard_map/psum | solution.py:118
  568.6 6.0 fusion.127
  574.6 40.4 %psum.190 = f32[4]{0:T(128)S(1)} all-reduce(f32[4]{0:T(128)} %get-tuple-element.99), channel_id=1, replica_groups=mesh['slab'=16,'grp'=8] {'slab'}, use_global_device_ids=true, to_apply=%region_30.31 | all-reduce | flops 4 | bytes 32 | tf_op jit(solution)/shard_map/psum | solution.py:88
  631.7 51.4 %all-reduce.37.cloned.1.call-done = (f32[4,4,32,256]{3,0,2,1:T(4,128)}, f32[4,32,256]{2,1,0:T(8,128)}) async-done(((f32[4,4,32,256]{3,0,2,1:T(4,128)}, f32[4,32,256]{2,1,0:T(8,128)}), (f32[4,4,32,256]{3,0,2,1:T(4,128)}, f32[4,32,256]{2,1,0:T(8,128)})) %all-reduce.37.cloned.1.call-update) | async-done | bytes 655376 | tf_op jit(solution)/shard_map/psum | solution.py:118
  683.1 5.8 fusion.128
  688.9 40.8 %psum.193 = f32[4]{0:T(128)S(1)} all-reduce(f32[4]{0:T(128)} %get-tuple-element.101), channel_id=1, replica_groups=mesh['slab'=16,'grp'=8] {'slab'}, use_global_device_ids=true, to_apply=%region_35.36 | all-reduce | flops 4 | bytes 32 | tf_op jit(solution)/shard_map/psum | solution.py:88
  744.0 52.3 %all-reduce.35.cloned.1.call-done = (f32[4,4,32,256]{3,0,2,1:T(4,128)}, f32[4,32,256]{2,1,0:T(8,128)}) async-done(((f32[4,4,32,256]{3,0,2,1:T(4,128)}, f32[4,32,256]{2,1,0:T(8,128)}), (f32[4,4,32,256]{3,0,2,1:T(4,128)}, f32[4,32,256]{2,1,0:T(8,128)})) %all-reduce.35.cloned.1.call-update) | async-done | bytes 655376 | tf_op jit(solution)/shard_map/psum | solution.py:118
  796.3 5.8 fusion.129
  802.1 40.4 %psum.196 = f32[4]{0:T(128)S(1)} all-reduce(f32[4]{0:T(128)} %get-tuple-element.103), channel_id=1, replica_groups=mesh['slab'=16,'grp'=8] {'slab'}, use_global_device_ids=true, to_apply=%region_40.41 | all-reduce | flops 4 | bytes 32 | tf_op jit(solution)/shard_map/psum | solution.py:88
  851.1 62.5 %psum.199 = f32[4,4]{1,0:T(4,128)S(1)} all-reduce(f32[4,4]{1,0:T(4,128)S(1)} %convolution_add_fusion), channel_id=1, replica_groups=mesh['slab'=16,'grp'=8] {'slab','grp'}, use_global_device_ids=true, to_apply=%region_44.45 | all-reduce | flops 16 | bytes 128 | tf_op jit(solution)/shard_map/psum | solution.py:159
  917.6 4.4 collective-permute-done.14
  922.6 56.6 %all-reduce.33.cloned.1.call-done = (f32[4,4,32,256]{3,0,2,1:T(4,128)}, f32[4,32,256]{2,1,0:T(8,128)}) async-done(((f32[4,4,32,256]{3,0,2,1:T(4,128)}, f32[4,32,256]{2,1,0:T(8,128)}), (f32[4,4,32,256]{3,0,2,1:T(4,128)}, f32[4,32,256]{2,1,0:T(8,128)})) %all-reduce.33.cloned.1.call-update) | async-done | bytes 655376 | tf_op jit(solution)/shard_map/psum | solution.py:118
  (217 shorter events, 130.4 us)
Async XLA Ops:
  7.2 73.3 %all-reduce.25.cloned.1.call-start = ((), (), s32[]{:S(2)}) async-start(), calls=%async_computation | async-start | bytes 1048576 | tf_op jit(solution)/shard_map/psum | solution.py:46
  8.7 10.6 %collective-permute-start.1 = (f32[4,1,32,256]{3,0,2,1:T(4,128)S(1)}, f32[4,1,32,256]{3,0,2,1:T(4,128)S(1)}, u32[]{:S(2)}, u32[]{:S(2)}) collective-permute-start(f32[4,1,32,256]{3,0,2,1:T(4,128)S(1)} %get-tuple-element.71), channel_id=1, source_target_pairs={{0,8},{8,16},{16,24},{24,32},{32,40},{40,48},{48,56},{56,64},{64,7... | collective-permute-start | bytes 393224 | tf_op jit(solution)/shard_map/ppermute | solution.py:20
  12.4 7.0 collective-permute-start
  15.5 174.8 %all-reduce.27.cloned.1.call-start = ((), (), s32[]{:S(2)}) async-start(), calls=%async_computation.1 | async-start | bytes 1048576 | tf_op jit(solution)/shard_map/psum | solution.py:46
  128.3 4.3 collective-permute-start.3
  129.6 6.9 collective-permute-start.2
  132.6 167.1 %all-reduce.29.cloned.1.call-start = ((), (), s32[]{:S(2)}) async-start(), calls=%async_computation.2 | async-start | bytes 1048576 | tf_op jit(solution)/shard_map/psum | solution.py:46
  237.8 4.5 collective-permute-start.5
  239.1 6.9 collective-permute-start.4
  242.0 169.3 %all-reduce.31.cloned.1.call-start = ((), (), s32[]{:S(2)}) async-start(), calls=%async_computation.3 | async-start | bytes 1048576 | tf_op jit(solution)/shard_map/psum | solution.py:46
  349.4 4.3 collective-permute-start.7
  350.7 7.1 collective-permute-start.6
  353.6 215.0 %all-reduce.39.cloned.1.call-start = ((), (), s32[]{:S(2)}) async-start(), calls=%async_computation.7 | async-start | bytes 1310720 | tf_op jit(solution)/shard_map/psum | solution.py:118
  501.9 13.6 %collective-permute-start.9 = (f32[4,1,32,256]{3,0,2,1:T(4,128)}, f32[4,1,32,256]{3,0,2,1:T(4,128)}, u32[]{:S(2)}, u32[]{:S(2)}) collective-permute-start(f32[4,1,32,256]{3,0,2,1:T(4,128)} %get-tuple-element.63), channel_id=1, source_target_pairs={{0,8},{8,16},{16,24},{24,32},{32,40},{40,48},{48,56},{56,64},{64,7... | collective-permute-start | bytes 393224 | tf_op jit(solution)/shard_map/ppermute | solution.py:20
  506.4 9.0 collective-permute-start.8
  510.7 172.4 %all-reduce.37.cloned.1.call-start = ((), (), s32[]{:S(2)}) async-start(), calls=%async_computation.6 | async-start | bytes 1310720 | tf_op jit(solution)/shard_map/psum | solution.py:118
  619.5 9.5 collective-permute-start.11
  621.4 7.5 collective-permute-start.10
  624.8 171.5 %all-reduce.35.cloned.1.call-start = ((), (), s32[]{:S(2)}) async-start(), calls=%async_computation.5 | async-start | bytes 1310720 | tf_op jit(solution)/shard_map/psum | solution.py:118
  733.2 9.0 collective-permute-start.13
  734.7 7.6 collective-permute-start.12
  738.0 241.2 %all-reduce.33.cloned.1.call-start = ((), (), s32[]{:S(2)}) async-start(), calls=%async_computation.4 | async-start | bytes 1310720 | tf_op jit(solution)/shard_map/psum | solution.py:118
  913.7 3.9 collective-permute-start.15
  915.0 7.0 collective-permute-start.14
  (51 other events, 1478.6 us)
Sparse Core Ops, SparseCore 0:
  15.7 64.7 all-reduce.24
  132.7 57.5 all-reduce.26
  242.1 57.5 all-reduce.28
  353.7 57.5 all-reduce.30
  510.8 57.7 all-reduce.38
  624.9 58.1 all-reduce.36
  738.1 58.1 all-reduce.34
  916.5 62.6 all-reduce.32
where the time goes:
time: 999 us; the launch traced here: 990 us
  waiting for transfers between devices  444 us (44%)
  blocking collectives  381 us (38%)
  matrix products  68.3 us (7%)
  other arithmetic  46.8 us (5%)
  starting transfers between devices  27.8 us (3%)
  between operations  15 us (2%)
    psum x4, waiting for transfers between devices, advance_local(): class_sums = lax.psum(partial_sums, 'grp')  216 us
    psum x4, waiting for transfers between devices, retreat(): weighted_sums, shared_sum = lax.psum((weighted_sums, shared_sum), 'grp')  211 us
    psum x4, blocking collectives, advance_local(): lax.psum((jnp.sum(weighted * potential, axis=(1, 2, 3)), jnp.sum(weighted...  162 us
    psum x4, blocking collectives, retreat(): lagrange_adj = lax.psum(jnp.sum(first_part, axis=(1, 2, 3)), 'slab')  157 us
    psum x1, blocking collectives, on_device(): mobility_total = lax.psum(mobility_acc, ('slab', 'grp'))  62.5 us
    dot_general x4, matrix products, retreat(): jnp.einsum('pk,kxzy->pxzy', member, class_adj, precision=lax.Precision.HI...  20.6 us
  transfers between devices with their start and end apart: 24, of which 13 were waited for; matrix products, arithmetic and copies ran while one was open for 4% of the time, Pallas kernels for 0%

commit v1 on v0

--- a/solution.py
+++ b/solution.py
@@ -43,7 +43,7 @@
 def advance_local(fields, pair_rates, member, active):
     squared = fields * fields
     partial_sums = jnp.einsum("pk,pxzy->kxzy", member, squared, precision=lax.Precision.HIGHEST)
-    class_sums = lax.psum(partial_sums, "grp")
+    class_sums = jnp.sum(lax.all_gather(partial_sums, "grp"), axis=0)
     summed = jnp.sum(class_sums, axis=0)
     inverse = 1.0 / (1.0 + summed)
     driving = jnp.einsum("pk,kxzy->pxzy", pair_rates, class_sums, precision=lax.Precision.HIGHEST)

time: 999 us -> 886 us (0.89)
  waiting for transfers between devices: 444 us -> 323 us
  other arithmetic: 46.8 us -> 59.7 us
    psum x4 -> x0, waiting for transfers between devices: 216 us -> none  [advance_local(): class_sums = lax.psum(partial_sums, 'grp')]
    all_gather x0 -> x4, waiting for transfers between devices: none -> 74.4 us  [advance_local(): class_sums = jnp.sum(lax.all_gather(partial_sums, 'grp'), axis=0)]
    ppermute x8, waiting for transfers between devices: 15.9 us -> 33.9 us  [extended_2(): lax.ppermute(head, axis, [((i + 1) % count, i) for i in range(ends)])]
    reduce_sum x0 -> x4, other arithmetic: none -> 10.5 us  [advance_local(): class_sums = jnp.sum(lax.all_gather(partial_sums, 'grp'), axis=0)]
  transfers between devices with their start and end apart: 24 -> 24, of which waited for: 13 -> 22; matrix products, arithmetic and copies ran while one was open for 4% -> 2% of each run, Pallas kernels for 0% -> 0%
where the time goes in v1:
time: 886 us; the launch traced here: 877 us
  blocking collectives  381 us (43%)
  waiting for transfers between devices  323 us (36%)
  matrix products  64.6 us (7%)
  other arithmetic  59.7 us (7%)
  starting transfers between devices  26.5 us (3%)
  between operations  15.2 us (2%)
    psum x4, waiting for transfers between devices, retreat(): weighted_sums, shared_sum = lax.psum((weighted_sums, shared_sum), 'grp')  211 us
    psum x4, blocking collectives, advance_local(): lax.psum((jnp.sum(weighted * potential, axis=(1, 2, 3)), jnp.sum(weighted...  162 us
    psum x4, blocking collectives, retreat(): lagrange_adj = lax.psum(jnp.sum(first_part, axis=(1, 2, 3)), 'slab')  157 us
    all_gather x4, waiting for transfers between devices, advance_local(): class_sums = jnp.sum(lax.all_gather(partial_sums, 'grp'), axis=0)  74.4 us
    psum x1, blocking collectives, on_device(): mobility_total = lax.psum(mobility_acc, ('slab', 'grp'))  62.4 us
    ppermute x8, waiting for transfers between devices, extended_2(): lax.ppermute(head, axis, [((i + 1) % count, i) for i in range(ends)])  33.9 us
    dot_general x4, matrix products, retreat(): jnp.einsum('pk,kxzy->pxzy', member, class_adj, precision=lax.Precision.HI...  21 us
  transfers between devices with their start and end apart: 24, of which 22 were waited for; matrix products, arithmetic and copies ran while one was open for 2% of the time, Pallas kernels for 0%

profile of v1, /device:TPU:0, one launch (start us, length us, event | category | flops | bytes accessed | tf_op | source)
XLA Modules:
  0.0 876.5 jit_solution(2647473602031020269)
XLA Ops:
  22.9 22.3 %all-gather.9.cloned.1.call-done = f32[32,4,32,256]{3,2,1,0:T(8,128)} async-done(((f32[4,4,32,256]{3,2,1,0:T(8,128)}), f32[32,4,32,256]{3,2,1,0:T(8,128)}) %all-gather.9.cloned.1.call-update) | async-done | bytes 4194320 | tf_op jit(solution)/shard_map/all_gather | solution.py:46
  55.2 40.3 %all-reduce.11 = (f32[4]{0:T(128)S(1)}, f32[4]{0:T(128)S(1)}) all-reduce(f32[4]{0:T(128)S(1)} %get-tuple-element.19, f32[4]{0:T(128)S(1)} %get-tuple-element.18), channel_id=1, replica_groups=mesh['slab'=16,'grp'=8] {'slab'}, use_global_device_ids=true, to_apply=%region_3.4 | all-reduce | flops 8 | bytes 64 | tf_op jit(solution)/shard_map/psum | solution.py:59
  101.9 4.4 collective-permute-done.2
  108.0 17.4 %all-gather.11.cloned.1.call-done = f32[32,4,32,256]{3,2,1,0:T(8,128)} async-done(((f32[4,4,32,256]{3,2,1,0:T(8,128)}), f32[32,4,32,256]{3,2,1,0:T(8,128)}) %all-gather.11.cloned.1.call-update) | async-done | bytes 4194320 | tf_op jit(solution)/shard_map/all_gather | solution.py:46
  135.4 40.3 %all-reduce.10 = (f32[4]{0:T(128)S(1)}, f32[4]{0:T(128)S(1)}) all-reduce(f32[4]{0:T(128)S(1)} %get-tuple-element.17, f32[4]{0:T(128)S(1)} %get-tuple-element.16), channel_id=1, replica_groups=mesh['slab'=16,'grp'=8] {'slab'}, use_global_device_ids=true, to_apply=%region_9.10 | all-reduce | flops 8 | bytes 64 | tf_op jit(solution)/shard_map/psum | solution.py:59
  187.9 17.4 %all-gather.13.cloned.1.call-done = f32[32,4,32,256]{3,2,1,0:T(8,128)} async-done(((f32[4,4,32,256]{3,2,1,0:T(8,128)}), f32[32,4,32,256]{3,2,1,0:T(8,128)}) %all-gather.13.cloned.1.call-update) | async-done | bytes 4194320 | tf_op jit(solution)/shard_map/all_gather | solution.py:46
  211.3 4.5 fusion.148
  215.8 40.4 %all-reduce.9 = (f32[4]{0:T(128)S(1)}, f32[4]{0:T(128)S(1)}) all-reduce(f32[4]{0:T(128)} %get-tuple-element.15, f32[4]{0:T(128)S(1)} %get-tuple-element.14), channel_id=1, replica_groups=mesh['slab'=16,'grp'=8] {'slab'}, use_global_device_ids=true, to_apply=%region_15.16 | all-reduce | flops 8 | bytes 64 | tf_op jit(solution)/shard_map/psum | solution.py:59
  269.9 17.4 %all-gather.15.cloned.1.call-done = f32[32,4,32,256]{3,2,1,0:T(8,128)} async-done(((f32[4,4,32,256]{3,2,1,0:T(8,128)}), f32[32,4,32,256]{3,2,1,0:T(8,128)}) %all-gather.15.cloned.1.call-update) | async-done | bytes 4194320 | tf_op jit(solution)/shard_map/all_gather | solution.py:46
  293.2 5.2 fusion.149
  298.5 40.4 %all-reduce.8 = (f32[4]{0:T(128)S(1)}, f32[4]{0:T(128)S(1)}) all-reduce(f32[4]{0:T(128)} %get-tuple-element.13, f32[4]{0:T(128)S(1)} %get-tuple-element.12), channel_id=1, replica_groups=mesh['slab'=16,'grp'=8] {'slab'}, use_global_device_ids=true, to_apply=%region_21.22 | all-reduce | flops 8 | bytes 64 | tf_op jit(solution)/shard_map/psum | solution.py:59
  342.3 35.7 %psum.155 = f32[4]{0:T(128)S(1)} all-reduce(f32[4]{0:T(128)S(1)} %get-tuple-element.54), channel_id=1, replica_groups=mesh['slab'=16,'grp'=8] {'slab'}, use_global_device_ids=true, to_apply=%region_25.26 | all-reduce | flops 4 | bytes 32 | tf_op jit(solution)/shard_map/psum | solution.py:88
  398.2 52.7 %all-reduce.27.cloned.1.call-done = (f32[4,4,32,256]{3,0,2,1:T(4,128)}, f32[4,32,256]{2,1,0:T(8,128)}) async-done(((f32[4,4,32,256]{3,0,2,1:T(4,128)}, f32[4,32,256]{2,1,0:T(8,128)}), (f32[4,4,32,256]{3,0,2,1:T(4,128)}, f32[4,32,256]{2,1,0:T(8,128)})) %all-reduce.27.cloned.1.call-update) | async-done | bytes 655376 | tf_op jit(solution)/shard_map/psum | solution.py:118
  451.0 6.0 fusion.139
  457.0 40.4 %psum.158 = f32[4]{0:T(128)S(1)} all-reduce(f32[4]{0:T(128)} %get-tuple-element.105), channel_id=1, replica_groups=mesh['slab'=16,'grp'=8] {'slab'}, use_global_device_ids=true, to_apply=%region_30.31 | all-reduce | flops 4 | bytes 32 | tf_op jit(solution)/shard_map/psum | solution.py:88
  515.6 51.0 %all-reduce.25.cloned.1.call-done = (f32[4,4,32,256]{3,0,2,1:T(4,128)}, f32[4,32,256]{2,1,0:T(8,128)}) async-done(((f32[4,4,32,256]{3,0,2,1:T(4,128)}, f32[4,32,256]{2,1,0:T(8,128)}), (f32[4,4,32,256]{3,0,2,1:T(4,128)}, f32[4,32,256]{2,1,0:T(8,128)})) %all-reduce.25.cloned.1.call-update) | async-done | bytes 655376 | tf_op jit(solution)/shard_map/psum | solution.py:118
  566.7 5.9 fusion.140
  572.6 40.4 %psum.161 = f32[4]{0:T(128)S(1)} all-reduce(f32[4]{0:T(128)} %get-tuple-element.107), channel_id=1, replica_groups=mesh['slab'=16,'grp'=8] {'slab'}, use_global_device_ids=true, to_apply=%region_35.36 | all-reduce | flops 4 | bytes 32 | tf_op jit(solution)/shard_map/psum | solution.py:88
  625.2 4.4 collective-permute-done.12
  631.3 51.1 %all-reduce.23.cloned.1.call-done = (f32[4,4,32,256]{3,0,2,1:T(4,128)}, f32[4,32,256]{2,1,0:T(8,128)}) async-done(((f32[4,4,32,256]{3,0,2,1:T(4,128)}, f32[4,32,256]{2,1,0:T(8,128)}), (f32[4,4,32,256]{3,0,2,1:T(4,128)}, f32[4,32,256]{2,1,0:T(8,128)})) %all-reduce.23.cloned.1.call-update) | async-done | bytes 655376 | tf_op jit(solution)/shard_map/psum | solution.py:118
  682.4 5.9 fusion.141
  688.3 40.6 %psum.164 = f32[4]{0:T(128)S(1)} all-reduce(f32[4]{0:T(128)} %get-tuple-element.109), channel_id=1, replica_groups=mesh['slab'=16,'grp'=8] {'slab'}, use_global_device_ids=true, to_apply=%region_40.41 | all-reduce | flops 4 | bytes 32 | tf_op jit(solution)/shard_map/psum | solution.py:88
  737.5 62.4 %psum.167 = f32[4,4]{1,0:T(4,128)S(1)} all-reduce(f32[4,4]{1,0:T(4,128)S(1)} %convolution_add_fusion), channel_id=1, replica_groups=mesh['slab'=16,'grp'=8] {'slab','grp'}, use_global_device_ids=true, to_apply=%region_44.45 | all-reduce | flops 16 | bytes 128 | tf_op jit(solution)/shard_map/psum | solution.py:159
  808.9 56.5 %all-reduce.21.cloned.1.call-done = (f32[4,4,32,256]{3,0,2,1:T(4,128)}, f32[4,32,256]{2,1,0:T(8,128)}) async-done(((f32[4,4,32,256]{3,0,2,1:T(4,128)}, f32[4,32,256]{2,1,0:T(8,128)}), (f32[4,4,32,256]{3,0,2,1:T(4,128)}, f32[4,32,256]{2,1,0:T(8,128)})) %all-reduce.21.cloned.1.call-update) | async-done | bytes 655376 | tf_op jit(solution)/shard_map/psum | solution.py:118
  (245 shorter events, 158.3 us)
Async XLA Ops:
  7.2 38.0 %all-gather.9.cloned.1.call-start = ((), (), s32[]{:S(2)}) async-start(), calls=%async_computation | async-start | bytes 4718592 | tf_op jit(solution)/shard_map/all_gather | solution.py:46
  10.3 115.1 %all-gather.11.cloned.1.call-start = ((), (), s32[]{:S(2)}) async-start(), calls=%async_computation.1 | async-start | bytes 4718592 | tf_op jit(solution)/shard_map/all_gather | solution.py:46
  10.7 6.3 collective-permute-start.1
  14.3 6.9 collective-permute-start
  98.0 107.2 %all-gather.13.cloned.1.call-start = ((), (), s32[]{:S(2)}) async-start(), calls=%async_computation.2 | async-start | bytes 4718592 | tf_op jit(solution)/shard_map/all_gather | solution.py:46
  98.1 3.8 collective-permute-start.3
  99.4 6.9 collective-permute-start.2
  177.9 109.3 %all-gather.15.cloned.1.call-start = ((), (), s32[]{:S(2)}) async-start(), calls=%async_computation.3 | async-start | bytes 4718592 | tf_op jit(solution)/shard_map/all_gather | solution.py:46
  178.0 3.8 collective-permute-start.5
  179.3 6.9 collective-permute-start.4
  259.9 191.1 %all-reduce.27.cloned.1.call-start = ((), (), s32[]{:S(2)}) async-start(), calls=%async_computation.7 | async-start | bytes 1310720 | tf_op jit(solution)/shard_map/psum | solution.py:118
  259.9 3.8 collective-permute-start.7
  261.3 6.9 collective-permute-start.6
  385.7 7.1 collective-permute-start.9
  389.6 6.9 collective-permute-start.8
  391.9 174.8 %all-reduce.25.cloned.1.call-start = ((), (), s32[]{:S(2)}) async-start(), calls=%async_computation.6 | async-start | bytes 1310720 | tf_op jit(solution)/shard_map/psum | solution.py:118
  505.7 3.9 collective-permute-start.11
  507.1 6.9 collective-permute-start.10
  508.4 174.0 %all-reduce.23.cloned.1.call-start = ((), (), s32[]{:S(2)}) async-start(), calls=%async_computation.5 | async-start | bytes 1310720 | tf_op jit(solution)/shard_map/psum | solution.py:118
  621.4 3.8 collective-permute-start.13
  622.7 6.9 collective-permute-start.12
  624.1 241.4 %all-reduce.21.cloned.1.call-start = ((), (), s32[]{:S(2)}) async-start(), calls=%async_computation.4 | async-start | bytes 1310720 | tf_op jit(solution)/shard_map/psum | solution.py:118
  799.9 3.9 collective-permute-start.15
  801.2 7.0 collective-permute-start.14
  (61 other events, 1623.1 us)
Sparse Core Ops, SparseCore 0:
  10.4 34.7 all-gather.8
  98.1 27.1 all-gather.10
  178.0 27.1 all-gather.12
  260.0 27.1 all-gather.14
  392.0 58.9 all-reduce.26
  508.5 58.0 all-reduce.24
  624.2 58.1 all-reduce.22
  802.7 62.6 all-reduce.20
